TPU v7x, 32 devices: a whole 2x2x4 slice. The times are simulated.
32 devices in a mesh: shard: 4 (over x, core), rep: 8 (over z, y).
Axes of the slice: x: 2, y: 2, z: 4, core: 2. Of those that a mesh axis runs over, the one named last changes fastest.
Arguments:
- tokens: bfloat16 [8, 512, 1024], P('rep', 'shard'), may hold values from -6 to 6
- cotangent: bfloat16 [8, 512, 1024], P('rep', 'shard'), may hold values from -6 to 6
- segment_ids: int32 [8, 512], P('rep'), may hold values from 0 to 3, never falling along the last dimension, each value on 1 to 256 neighbouring positions
- intake: float32 [3, 1024, 1024], P(None, ('shard', 'rep')), may hold values from -0.1875 to 0.1875
- outlet: float32 [1024, 1024], P(('shard', 'rep')), may hold values from -1.5 to 1.5
- expand: float32 [4096, 1024], P(('shard', 'rep')), may hold values from -0.1875 to 0.1875
- shrink: float32 [4096, 1024], P(('shard', 'rep')), may hold values from -0.09375 to 0.09375
- affine: float32 [8, 1024], P(None, ('shard', 'rep')), may hold values from -0.8 to 0.8
- offset: float32 [4096], P(('shard', 'rep')), may hold values from -0.8 to 0.8
- intake_first: float32 [3, 1024, 1024], P(None, ('shard', 'rep')), may hold values from -15 to 15
- outlet_first: float32 [1024, 1024], P(('shard', 'rep')), may hold values from -15 to 15
- expand_first: float32 [4096, 1024], P(('shard', 'rep')), may hold values from -15 to 15
- shrink_first: float32 [4096, 1024], P(('shard', 'rep')), may hold values from -15 to 15
- affine_first: float32 [8, 1024], P(None, ('shard', 'rep')), may hold values from -15 to 15
- offset_first: float32 [4096], P(('shard', 'rep')), may hold values from -15 to 15
- intake_second: float32 [3, 1024, 1024], P(None, ('shard', 'rep')), may hold values from 1 to 100
- outlet_second: float32 [1024, 1024], P(('shard', 'rep')), may hold values from 1 to 100
- expand_second: float32 [4096, 1024], P(('shard', 'rep')), may hold values from 1 to 100
- shrink_second: float32 [4096, 1024], P(('shard', 'rep')), may hold values from 1 to 100
- affine_second: float32 [8, 1024], P(None, ('shard', 'rep')), may hold values from 1 to 100
- offset_second: float32 [4096], P(('shard', 'rep')), may hold values from 1 to 100
Outputs:
- layer_out: bfloat16 [8, 512, 1024], P('rep', 'shard')
- token_grad: bfloat16 [8, 512, 1024], P('rep', 'shard')
- intake_grad: float32 [3, 1024, 1024], P(None, ('shard', 'rep'))
- outlet_grad: float32 [1024, 1024], P(('shard', 'rep'))
- expand_grad: float32 [4096, 1024], P(('shard', 'rep'))
- shrink_grad: float32 [4096, 1024], P(('shard', 'rep'))
- affine_grad: float32 [8, 1024], P(None, ('shard', 'rep'))
- offset_grad: float32 [4096], P(('shard', 'rep'))
- intake_next: float32 [3, 1024, 1024], P(None, ('shard', 'rep'))
- outlet_next: float32 [1024, 1024], P(('shard', 'rep'))
- expand_next: float32 [4096, 1024], P(('shard', 'rep'))
- shrink_next: float32 [4096, 1024], P(('shard', 'rep'))
- affine_next: float32 [8, 1024], P(None, ('shard', 'rep'))
- offset_next: float32 [4096], P(('shard', 'rep'))
- intake_momentum: float32 [3, 1024, 1024], P(None, ('shard', 'rep'))
- outlet_momentum: float32 [1024, 1024], P(('shard', 'rep'))
- expand_momentum: float32 [4096, 1024], P(('shard', 'rep'))
- shrink_momentum: float32 [4096, 1024], P(('shard', 'rep'))
- affine_momentum: float32 [8, 1024], P(None, ('shard', 'rep'))
- offset_momentum: float32 [4096], P(('shard', 'rep'))
- intake_variance: float32 [3, 1024, 1024], P(None, ('shard', 'rep'))
- outlet_variance: float32 [1024, 1024], P(('shard', 'rep'))
- expand_variance: float32 [4096, 1024], P(('shard', 'rep'))
- shrink_variance: float32 [4096, 1024], P(('shard', 'rep'))
- affine_variance: float32 [8, 1024], P(None, ('shard', 'rep'))
- offset_variance: float32 [4096], P(('shard', 'rep'))
Inputs may be any that keep to these rules, and one draw needn't show every extreme that they name: `segment_ids`: within each sequence the numbers never fall along positions, every number appears, each document spans at most 256 positions and one spans exactly that many.
All inputs are finite; a program needn't handle non-finite values.
Results may differ from a plain program's by a relative error of at most 0.025.
Values may be sent and summed in bfloat16 or wider, within the bound.
No kernel may reach another device: no remote copies, remote signals or barrier semaphores. Data moves between devices by JAX's collectives and lax.ppermute only.
A program may use at most 128 MiB of HBM per device.

v0:
```python
import math
import jax
import jax.numpy as jnp
from jax import lax
from jax.sharding import PartitionSpec as P

HEAD_DIM = 64
lr_rate = 0.03
beta_one = 0.9
beta_two = 0.95
adam_eps = 1e-08
weight_decay = 0.1
step_count = 3
norm_eps = 1e-05


def layer_norm(values_in):
    centred = values_in - jnp.mean(values_in, axis=-1, keepdims=True)
    inv_std = lax.rsqrt(jnp.mean(centred * centred, axis=-1, keepdims=True) + norm_eps)
    return (centred * inv_std, inv_std)


def norm_back(grad_normed, normed, inv_std):
    return inv_std * (
        grad_normed
        - jnp.mean(grad_normed, axis=-1, keepdims=True)
        - normed * jnp.mean(grad_normed * normed, axis=-1, keepdims=True)
    )


def gelu_value(hidden):
    return 0.5 * hidden * (1.0 + jax.scipy.special.erf(hidden / math.sqrt(2.0)))


def gelu_slope(hidden):
    return 0.5 * (1.0 + jax.scipy.special.erf(hidden / math.sqrt(2.0))) + hidden * jnp.exp(
        -0.5 * hidden * hidden
    ) / math.sqrt(2.0 * math.pi)


def adamw_step(weight, first_mom, second_mom, gradient):
    momentum = beta_one * first_mom + (1.0 - beta_one) * gradient
    variance = beta_two * second_mom + (1.0 - beta_two) * gradient * gradient
    fixed_mom = momentum / (1.0 - beta_one**step_count)
    fixed_var = variance / (1.0 - beta_two**step_count)
    return (
        weight - lr_rate * (fixed_mom / (jnp.sqrt(fixed_var) + adam_eps) + weight_decay * weight),
        momentum,
        variance,
    )


def plain_dot(left_side, right_side):
    return jnp.dot(left_side, right_side, preferred_element_type=jnp.float32)


def dot_rows(left_side, right_side):
    return lax.dot_general(
        left_side, right_side, (((1,), (1,)), ((), ())), preferred_element_type=jnp.float32
    )


def dot_cols(left_side, right_side):
    return lax.dot_general(
        left_side, right_side, (((0,), (0,)), ((), ())), preferred_element_type=jnp.float32
    )


def split_heads(values_in):
    return values_in.reshape(values_in.shape[0], values_in.shape[1] // HEAD_DIM, HEAD_DIM)


def attend_forward(query_half, key_half, value_half, same_doc):
    score_scale = 1.0 / math.sqrt(HEAD_DIM)
    scores = (
        jnp.einsum(
            "qhd,khd->hqk",
            split_heads(query_half),
            split_heads(key_half),
            preferred_element_type=jnp.float32,
        )
        * score_scale
    )
    exp_scores = jnp.where(same_doc, jnp.exp(scores), 0.0)
    totals = jnp.sum(exp_scores, axis=-1, keepdims=True)
    log_total = jnp.log(totals)
    prob_half = (exp_scores / totals).astype(jnp.bfloat16)
    attended = jnp.einsum(
        "hqk,khd->qhd", prob_half, split_heads(value_half), preferred_element_type=jnp.float32
    )
    return (attended.reshape(query_half.shape).astype(jnp.bfloat16), log_total)


def attend_backward(query_half, key_half, value_half, attend_grad, log_total, same_doc):
    score_scale = 1.0 / math.sqrt(HEAD_DIM)
    query_heads = split_heads(query_half)
    key_heads = split_heads(key_half)
    grad_heads = split_heads(attend_grad)
    scores_again = (
        jnp.einsum("qhd,khd->hqk", query_heads, key_heads, preferred_element_type=jnp.float32)
        * score_scale
    )
    prob_again = jnp.where(same_doc, jnp.exp(scores_again - log_total), 0.0)
    prob_grad = jnp.einsum(
        "qhd,khd->hqk", grad_heads, split_heads(value_half), preferred_element_type=jnp.float32
    )
    row_dots = jnp.sum(prob_again * prob_grad, axis=-1, keepdims=True)
    score_half = (prob_again * (prob_grad - row_dots)).astype(jnp.bfloat16)
    query_grad = (
        jnp.einsum("hqk,khd->qhd", score_half, key_heads, preferred_element_type=jnp.float32)
        * score_scale
    ).reshape(query_half.shape)
    key_terms = (
        jnp.einsum("hqk,qhd->khd", score_half, query_heads, preferred_element_type=jnp.float32)
        * score_scale
    ).reshape(key_half.shape)
    value_terms = jnp.einsum(
        "hqk,qhd->khd",
        prob_again.astype(jnp.bfloat16),
        grad_heads,
        preferred_element_type=jnp.float32,
    ).reshape(key_half.shape)
    return (query_grad, key_terms, value_terms)


def body(
    tokens,
    cotangent,
    segment_ids,
    intake,
    outlet,
    expand,
    shrink,
    affine,
    offset,
    intake_first,
    outlet_first,
    expand_first,
    shrink_first,
    affine_first,
    offset_first,
    intake_second,
    outlet_second,
    expand_second,
    shrink_second,
    affine_second,
    offset_second,
):
    own_rows = tokens.shape[1]
    model_width = tokens.shape[2]
    groups = lax.axis_size("shard")
    position = lax.axis_index("shard")
    seq_len = own_rows * groups
    source = tokens.reshape(own_rows, model_width)
    every_seg = segment_ids.reshape(seq_len)
    own_seg = lax.dynamic_slice_in_dim(every_seg, position * own_rows, own_rows)
    part_intake, part_outlet, part_expand, part_shrink, part_affine, part_offset = (
        lax.all_gather(intake.astype(jnp.bfloat16), "rep", axis=1, tiled=True),
        lax.all_gather(outlet.astype(jnp.bfloat16), "rep", axis=0, tiled=True),
        lax.all_gather(expand.astype(jnp.bfloat16), "rep", axis=0, tiled=True),
        lax.all_gather(shrink.astype(jnp.bfloat16), "rep", axis=0, tiled=True),
        lax.all_gather(affine.astype(jnp.bfloat16), "rep", axis=1, tiled=True),
        lax.all_gather(offset.astype(jnp.bfloat16), "rep", axis=0, tiled=True),
    )

    def layer_params():
        return (
            lax.all_gather(part_intake, "shard", axis=1, tiled=True),
            lax.all_gather(part_outlet, "shard", axis=0, tiled=True),
            lax.all_gather(part_affine, "shard", axis=1, tiled=True),
            lax.all_gather(part_offset, "shard", axis=0, tiled=True),
        )

    full_intake, full_outlet, full_affine, full_offset = layer_params()
    coeffs = full_affine.astype(jnp.float32)
    query_half = (dot_rows(source, full_intake[0]) + coeffs[0]).astype(jnp.bfloat16)
    key_part = dot_rows(source, full_intake[1]).astype(jnp.bfloat16)
    value_part = (dot_rows(source, full_intake[2]) + coeffs[1]).astype(jnp.bfloat16)
    key_half, value_half = (
        lax.all_gather(key_part, "shard", axis=0, tiled=True),
        lax.all_gather(value_part, "shard", axis=0, tiled=True),
    )
    same_doc = (own_seg[:, None] == every_seg[None, :])[None]
    attended, log_total = attend_forward(query_half, key_half, value_half, same_doc)
    attn_out = plain_dot(attended, full_outlet)
    resid_one = source.astype(jnp.float32) + attn_out + coeffs[2]
    normed_one, inv_one = layer_norm(resid_one)
    mixed_one = normed_one * (1.0 + coeffs[3]) + coeffs[4]
    inner_in = mixed_one.astype(jnp.bfloat16)
    group_in = lax.all_gather(inner_in, "shard", axis=0, tiled=True)
    hidden = dot_rows(group_in, part_expand) + part_offset.astype(jnp.float32)
    act_half = gelu_value(hidden).astype(jnp.bfloat16)
    ffn_out = lax.psum_scatter(
        plain_dot(act_half, part_shrink).astype(jnp.bfloat16),
        "shard",
        scatter_dimension=0,
        tiled=True,
    ).astype(jnp.float32)
    resid_two = mixed_one + ffn_out + coeffs[5]
    normed_two, inv_two = layer_norm(resid_two)
    layer_out = (normed_two * (1.0 + coeffs[6]) + coeffs[7]).astype(jnp.bfloat16)
    back_intake, back_outlet, back_affine, back_offset = layer_params()
    back_coeffs = back_affine.astype(jnp.float32)
    out_grad = cotangent.reshape(own_rows, model_width).astype(jnp.float32)
    gain_two = jnp.sum(out_grad * normed_two, axis=0)
    shift_two = jnp.sum(out_grad, axis=0)
    grad_two = norm_back(out_grad * (1.0 + back_coeffs[6]), normed_two, inv_two)
    bias_two = jnp.sum(grad_two, axis=0)
    grad_half = grad_two.astype(jnp.bfloat16)
    group_grad = lax.all_gather(grad_half, "shard", axis=0, tiled=True)
    shrink_part = dot_cols(act_half, group_grad)
    grad_hidden = dot_rows(group_grad, part_shrink) * gelu_slope(hidden)
    slice_len = grad_hidden.shape[1]
    offset_full = lax.dynamic_update_slice(
        jnp.zeros((slice_len * groups,), jnp.float32),
        jnp.sum(grad_hidden, axis=0),
        (position * slice_len,),
    )
    hidden_half = grad_hidden.astype(jnp.bfloat16)
    expand_part = dot_cols(hidden_half, group_in)
    grad_inner = lax.psum_scatter(
        plain_dot(hidden_half, part_expand).astype(jnp.bfloat16),
        "shard",
        scatter_dimension=0,
        tiled=True,
    ).astype(jnp.float32)
    grad_mixed = grad_two + grad_inner
    gain_one = jnp.sum(grad_mixed * normed_one, axis=0)
    shift_one = jnp.sum(grad_mixed, axis=0)
    grad_one = norm_back(grad_mixed * (1.0 + back_coeffs[3]), normed_one, inv_one)
    bias_out = jnp.sum(grad_one, axis=0)
    one_half = grad_one.astype(jnp.bfloat16)
    outlet_full = dot_cols(attended, one_half)
    attend_grad = dot_rows(one_half, back_outlet).astype(jnp.bfloat16)
    query_grad, key_terms, value_terms = attend_backward(
        query_half, key_half, value_half, attend_grad, log_total, same_doc
    )
    key_grad, value_grad = (
        lax.psum_scatter(
            key_terms.astype(jnp.bfloat16), "shard", scatter_dimension=0, tiled=True
        ).astype(jnp.float32),
        lax.psum_scatter(
            value_terms.astype(jnp.bfloat16), "shard", scatter_dimension=0, tiled=True
        ).astype(jnp.float32),
    )
    query_low = query_grad.astype(jnp.bfloat16)
    key_low = key_grad.astype(jnp.bfloat16)
    value_low = value_grad.astype(jnp.bfloat16)
    intake_full = jnp.stack(
        [dot_cols(query_low, source), dot_cols(key_low, source), dot_cols(value_low, source)]
    )
    token_grad = (
        grad_one
        + plain_dot(query_low, back_intake[0])
        + plain_dot(key_low, back_intake[1])
        + plain_dot(value_low, back_intake[2])
    ).astype(jnp.bfloat16)
    affine_full = jnp.stack(
        [
            jnp.sum(query_grad, axis=0),
            jnp.sum(value_grad, axis=0),
            bias_out,
            gain_one,
            shift_one,
            bias_two,
            gain_two,
            shift_two,
        ]
    )
    intake_part, outlet_part, affine_part, offset_part = (
        lax.psum_scatter(
            intake_full.astype(jnp.bfloat16), "shard", scatter_dimension=1, tiled=True
        ).astype(jnp.float32),
        lax.psum_scatter(
            outlet_full.astype(jnp.bfloat16), "shard", scatter_dimension=0, tiled=True
        ).astype(jnp.float32),
        lax.psum_scatter(
            affine_full.astype(jnp.bfloat16), "shard", scatter_dimension=1, tiled=True
        ).astype(jnp.float32),
        lax.psum_scatter(
            offset_full.astype(jnp.bfloat16), "shard", scatter_dimension=0, tiled=True
        ).astype(jnp.float32),
    )
    intake_grad, outlet_grad, expand_grad, shrink_grad, affine_grad, offset_grad = (
        lax.psum_scatter(intake_part, "rep", scatter_dimension=1, tiled=True),
        lax.psum_scatter(outlet_part, "rep", scatter_dimension=0, tiled=True),
        lax.psum_scatter(expand_part, "rep", scatter_dimension=0, tiled=True),
        lax.psum_scatter(shrink_part, "rep", scatter_dimension=0, tiled=True),
        lax.psum_scatter(affine_part, "rep", scatter_dimension=1, tiled=True),
        lax.psum_scatter(offset_part, "rep", scatter_dimension=0, tiled=True),
    )
    intake_next, intake_momentum, intake_variance = adamw_step(
        intake, intake_first, intake_second, intake_grad
    )
    outlet_next, outlet_momentum, outlet_variance = adamw_step(
        outlet, outlet_first, outlet_second, outlet_grad
    )
    expand_next, expand_momentum, expand_variance = adamw_step(
        expand, expand_first, expand_second, expand_grad
    )
    shrink_next, shrink_momentum, shrink_variance = adamw_step(
        shrink, shrink_first, shrink_second, shrink_grad
    )
    affine_next, affine_momentum, affine_variance = adamw_step(
        affine, affine_first, affine_second, affine_grad
    )
    offset_next, offset_momentum, offset_variance = adamw_step(
        offset, offset_first, offset_second, offset_grad
    )
    return (
        layer_out.reshape(tokens.shape),
        token_grad.reshape(cotangent.shape),
        intake_grad,
        outlet_grad,
        expand_grad,
        shrink_grad,
        affine_grad,
        offset_grad,
        intake_next,
        outlet_next,
        expand_next,
        shrink_next,
        affine_next,
        offset_next,
        intake_momentum,
        outlet_momentum,
        expand_momentum,
        shrink_momentum,
        affine_momentum,
        offset_momentum,
        intake_variance,
        outlet_variance,
        expand_variance,
        shrink_variance,
        affine_variance,
        offset_variance,
    )


def solution(mesh):
    placed = (
        P("rep", "shard", None),
        P("rep", "shard", None),
        P("rep", None),
        P(None, ("shard", "rep"), None),
        P(("shard", "rep"), None),
        P(("shard", "rep"), None),
        P(("shard", "rep"), None),
        P(None, ("shard", "rep")),
        P(("shard", "rep")),
        P(None, ("shard", "rep"), None),
        P(("shard", "rep"), None),
        P(("shard", "rep"), None),
        P(("shard", "rep"), None),
        P(None, ("shard", "rep")),
        P(("shard", "rep")),
        P(None, ("shard", "rep"), None),
        P(("shard", "rep"), None),
        P(("shard", "rep"), None),
        P(("shard", "rep"), None),
        P(None, ("shard", "rep")),
        P(("shard", "rep")),
    )
    return jax.shard_map(
        body,
        mesh=mesh,
        in_specs=placed,
        out_specs=(
            P("rep", "shard", None),
            P("rep", "shard", None),
            P(None, ("shard", "rep"), None),
            P(("shard", "rep"), None),
            P(("shard", "rep"), None),
            P(("shard", "rep"), None),
            P(None, ("shard", "rep")),
            P(("shard", "rep")),
            P(None, ("shard", "rep"), None),
            P(("shard", "rep"), None),
            P(("shard", "rep"), None),
            P(("shard", "rep"), None),
            P(None, ("shard", "rep")),
            P(("shard", "rep")),
            P(None, ("shard", "rep"), None),
            P(("shard", "rep"), None),
            P(("shard", "rep"), None),
            P(("shard", "rep"), None),
            P(None, ("shard", "rep")),
            P(("shard", "rep")),
            P(None, ("shard", "rep"), None),
            P(("shard", "rep"), None),
            P(("shard", "rep"), None),
            P(("shard", "rep"), None),
            P(None, ("shard", "rep")),
            P(("shard", "rep")),
        ),
        check_vma=False,
    )
```

profile of v0, /device:TPU:0, one launch (start us, length us, event | category | flops | bytes accessed | tf_op | source)
XLA Modules:
  0.0 948.7 jit_solution(9092872579765308628)
XLA Ops:
  7.3 1.7 convert_element_type.149
  9.1 48.7 %all-gather.12.cloned.1.call-done = bf16[3,256,1024]{2,1,0:T(8,128)(2,1)} async-done(((bf16[3,32,1024]{2,1,0:T(8,128)(2,1)}), bf16[3,256,1024]{2,1,0:T(8,128)(2,1)}) %all-gather.12.cloned.1.call-update) | async-done | bytes 1572880 | tf_op jit(solution)/shard_map/all_gather | solution.py:158
  57.8 26.1 %all-gather = bf16[8,32,8]{1,2,0:T(8,128)(2,1)S(1)} all-gather(bf16[1,32,8]{1,2,0:T(8,128)(2,1)S(1)} %convert_bitcast_fusion.3), channel_id=1, replica_groups=mesh['shard'=4,'rep'=8] {'rep'}, dimensions={0}, use_global_device_ids=true | all-gather | bytes 4608 | tf_op jit(solution)/shard_map/all_gather | solution.py:162
  84.0 5.4 all_gather.45
  89.4 14.7 %all-gather.14.cloned.1.call-done = bf16[3,1024,1024]{2,1,0:T(8,128)(2,1)} async-done(((bf16[3,256,1024]{2,1,0:T(8,128)(2,1)}), bf16[3,1024,1024]{2,1,0:T(8,128)(2,1)}) %all-gather.14.cloned.1.call-update) | async-done | bytes 6291472 | tf_op jit(solution)/shard_map/all_gather | solution.py:168
  104.1 3.1 fusion.33
  107.3 3.2 fusion.31
  110.6 33.3 %all_gather.48 = bf16[256,1024]{1,0:T(8,128)(2,1)} all-gather(bf16[32,1024]{1,0:T(8,128)(2,1)S(1)} %convert_element_type.159), channel_id=1, replica_groups=mesh['shard'=4,'rep'=8] {'rep'}, dimensions={0}, use_global_device_ids=true | all-gather | bytes 589824 | tf_op jit(solution)/shard_map/all_gather | solution.py:159
  145.0 2.4 fusion.34
  147.7 1.6 copy.61
  149.3 1.9 copy.63
  152.4 2.0 copy-done
  154.5 1.3 fusion.32
  155.7 11.2 %all-gather.20.cloned.1.call-done = bf16[1024,1024]{1,0:T(8,128)(2,1)} async-done(((bf16[256,1024]{1,0:T(8,128)(2,1)}), bf16[1024,1024]{1,0:T(8,128)(2,1)}) %all-gather.20.cloned.1.call-update) | async-done | bytes 2097168 | tf_op jit(solution)/shard_map/all_gather | solution.py:169
  166.9 2.2 fusion.79
  171.1 20.5 %all-gather.1 = bf16[8,1,128]{2,1,0:T(2,128)(2,1)S(1)} all-gather(bf16[1,1,128]{2,1,0:T(2,128)(2,1)S(1)} %convert_bitcast_fusion.4), channel_id=1, replica_groups=mesh['shard'=4,'rep'=8] {'rep'}, dimensions={0}, use_global_device_ids=true | all-gather | bytes 2304 | tf_op jit(solution)/shard_map/all_gather | solution.py:163
  191.6 27.0 %all-gather.24.cloned.1.call-done = bf16[1024,1024]{1,0:T(8,128)(2,1)} async-done(((bf16[128,1024]{1,0:T(8,128)(2,1)}), bf16[1024,1024]{1,0:T(8,128)(2,1)}) %all-gather.24.cloned.1.call-update) | async-done | bytes 2097168 | tf_op jit(solution)/shard_map/all_gather | solution.py:160
  218.6 17.4 %all-gather.22.cloned.1.call-done = bf16[512,1024]{1,0:T(8,128)(2,1)} async-done(((bf16[128,1024]{1,0:T(8,128)(2,1)}), bf16[512,1024]{1,0:T(8,128)(2,1)}) %all-gather.22.cloned.1.call-update) | async-done | bytes 1048592 | tf_op jit(solution)/shard_map/all_gather | solution.py:190
  236.0 4.7 multiply_convert_fusion.2
  240.7 47.1 %all-gather.26.cloned.1.call-done = bf16[1024,1024]{1,0:T(8,128)(2,1)} async-done(((bf16[128,1024]{1,0:T(8,128)(2,1)}), bf16[1024,1024]{1,0:T(8,128)(2,1)}) %all-gather.26.cloned.1.call-update) | async-done | bytes 2097168 | tf_op jit(solution)/shard_map/all_gather | solution.py:161
  287.8 3.8 convolution_convert_fusion.2
  291.7 23.4 %reduce-scatter.19.cloned.1.call-done = bf16[128,1024]{1,0:T(8,128)(2,1)} async-done(((bf16[512,1024]{1,0:T(8,128)(2,1)}), bf16[128,1024]{1,0:T(8,128)(2,1)}) %reduce-scatter.19.cloned.1.call-update) | async-done | bytes 262160 | tf_op jit(solution)/shard_map/reduce_scatter | solution.py:193
  315.1 1.2 fusion.76
  318.2 16.6 %all-gather.28.cloned.1.call-done = bf16[512,1024]{1,0:T(8,128)(2,1)} async-done(((bf16[128,1024]{1,0:T(8,128)(2,1)}), bf16[512,1024]{1,0:T(8,128)(2,1)}) %all-gather.28.cloned.1.call-update) | async-done | bytes 1048592 | tf_op jit(solution)/shard_map/all_gather | solution.py:210
  334.9 4.6 fusion.80
  340.5 2.3 convolution_convert_fusion.1
  342.8 24.9 %reduce-scatter.21.cloned.1.call-done = bf16[128,1024]{1,0:T(8,128)(2,1)} async-done(((bf16[512,1024]{1,0:T(8,128)(2,1)}), bf16[128,1024]{1,0:T(8,128)(2,1)}) %reduce-scatter.21.cloned.1.call-update) | async-done | bytes 262160 | tf_op jit(solution)/shard_map/reduce_scatter | solution.py:221
  367.7 1.3 multiply_reduce_fusion.1
  369.0 1.3 fusion.73
  371.3 3.3 fusion.20
  374.6 1.3 copy.67
  376.1 3.5 multiply_reduce_fusion
  379.6 1.5 multiply_convert_fusion
  381.2 1.4 multiply_convert_fusion.1
  382.6 2.3 copy.65
  385.1 2.1 fusion.77
  387.3 13.6 %reduce-scatter.39.cloned.1.call-done = bf16[128,1024]{1,0:T(8,128)(2,1)} async-done(((bf16[512,1024]{1,0:T(8,128)(2,1)}), bf16[128,1024]{1,0:T(8,128)(2,1)}) %reduce-scatter.39.cloned.1.call-update) | async-done | bytes 262160
  402.7 2.0 convolution_convert_fusion
  405.7 2.1 convert_bitcast_fusion
  407.8 20.5 %reduce-scatter.37.cloned.1.call-done = bf16[128,1024]{1,0:T(8,128)(2,1)} async-done(((bf16[512,1024]{1,0:T(8,128)(2,1)}), bf16[128,1024]{1,0:T(8,128)(2,1)}) %reduce-scatter.37.cloned.1.call-update) | async-done | bytes 262160
  428.3 1.8 convert_bitcast_fusion.1
  430.1 3.3 pad_maximum_fusion
  433.5 17.2 %reduce-scatter.35.cloned.1.call-done = bf16[8,256]{1,0:T(8,128)(2,1)} async-done(((bf16[8,1024]{1,0:T(8,128)(2,1)}), bf16[8,256]{1,0:T(8,128)(2,1)}) %reduce-scatter.35.cloned.1.call-update) | async-done | bytes 4112 | tf_op jit(solution)/shard_map/reduce_scatter | solution.py:277
  450.7 1.4 copy.69
  452.2 32.1 %reduce-scatter.27.cloned.1.call-done = bf16[256,1024]{1,0:T(8,128)(2,1)} async-done(((bf16[1024,1024]{1,0:T(8,128)(2,1)}), bf16[256,1024]{1,0:T(8,128)(2,1)}) %reduce-scatter.27.cloned.1.call-update) | async-done | bytes 524304 | tf_op jit(solution)/shard_map/reduce_scatter | solution.py:274
  484.3 2.1 convert_element_type.190
  486.7 3.2 fusion.45
  491.5 3.3 fusion.81
  494.8 49.8 %reduce-scatter.23.cloned.1.call-done = bf16[3,256,1024]{2,1,0:T(8,128)(2,1)} async-done(((bf16[3,1024,1024]{2,1,0:T(8,128)(2,1)}), bf16[3,256,1024]{2,1,0:T(8,128)(2,1)}) %reduce-scatter.23.cloned.1.call-update) | async-done | bytes 1572880 | tf_op jit(solution)/shard_map/reduce_scatter | solution.py:271
  544.6 3.5 convert_element_type.188
  551.5 5.8 all-reduce
  557.4 21.6 %all-reduce.1 = f32[1024]{0:T(1024)S(1)} all-reduce(f32[1024]{0:T(1024)S(1)} %dynamic-slice_convert_fusion), channel_id=15, replica_groups=mesh['shard'=4,'rep'=8] {'rep'}, use_global_device_ids=true, to_apply=%region_32.33.clone | all-reduce | flops 1024 | bytes 8192
  579.6 2.1 fusion.27
  581.7 2.1 fusion.14
  583.9 2.9 fusion.35
  586.8 23.6 %reduce-scatter.41.cloned.1.call-done = f32[32,8]{1,0:T(8,128)} async-done(((f32[256,8]{1,0:T(8,128)}), f32[32,8]{1,0:T(8,128)}) %reduce-scatter.41.cloned.1.call-update) | async-done | bytes 1040
  611.7 65.7 %reduce-scatter.29.cloned.1.call-done = f32[32,1024]{1,0:T(8,128)} async-done(((f32[256,1024]{1,0:T(8,128)}), f32[32,1024]{1,0:T(8,128)}) %reduce-scatter.29.cloned.1.call-update) | async-done | bytes 131088 | tf_op jit(solution)/shard_map/reduce_scatter | solution.py:286
  677.4 1.8 multiply_subtract_fusion.3
  679.3 89.6 %reduce-scatter.31.cloned.1.call-done = f32[128,1024]{1,0:T(8,128)} async-done(((f32[1024,1024]{1,0:T(8,128)}), f32[128,1024]{1,0:T(8,128)}) %reduce-scatter.31.cloned.1.call-update) | async-done | bytes 524304 | tf_op jit(solution)/shard_map/reduce_scatter | solution.py:287
  768.9 2.4 multiply_subtract_fusion.1
  771.4 89.6 %reduce-scatter.33.cloned.1.call-done = f32[128,1024]{1,0:T(8,128)} async-done(((f32[1024,1024]{1,0:T(8,128)}), f32[128,1024]{1,0:T(8,128)}) %reduce-scatter.33.cloned.1.call-update) | async-done | bytes 524304 | tf_op jit(solution)/shard_map/reduce_scatter | solution.py:288
  861.0 2.4 multiply_subtract_fusion
  863.4 76.2 %reduce-scatter.25.cloned.1.call-done = f32[3,32,1024]{2,1,0:T(8,128)} async-done(((f32[3,256,1024]{2,1,0:T(8,128)}), f32[3,32,1024]{2,1,0:T(8,128)}) %reduce-scatter.25.cloned.1.call-update) | async-done | bytes 393232 | tf_op jit(solution)/shard_map/reduce_scatter | solution.py:285
  939.7 2.2 multiply_subtract_fusion.2
  (187 shorter events, 17.9 us)
Async XLA Ops:
  7.2 50.6 %copy-start.37 = (f32[8,32]{1,0:T(8,128)S(1)}, f32[8,32]{1,0:T(8,128)}, u32[]{:S(2)}) copy-start(f32[8,32]{1,0:T(8,128)} %param.28) | copy-start | bytes 3076
  7.2 96.9 %copy-start.7 = (bf16[1,128,1024]{2,1,0:T(8,128)(2,1)S(1)}, bf16[1,128,1024]{2,1,0:T(8,128)(2,1)}, u32[]{:S(2)}) copy-start(bf16[1,128,1024]{2,1,0:T(8,128)(2,1)} %param.21) | copy-start | bytes 786436
  7.2 50.5 %all-gather.12.cloned.1.call-start = ((), (), s32[]{:S(2)}) async-start(), calls=%async_computation.12 | async-start | bytes 1769472 | tf_op jit(solution)/shard_map/all_gather | solution.py:158
  9.0 95.1 %all-gather.14.cloned.1.call-start = ((), (), s32[]{:S(2)}) async-start(), calls=%async_computation.13 | async-start | bytes 7864320 | tf_op jit(solution)/shard_map/all_gather | solution.py:168
  57.8 89.9 %all-gather.16.cloned.1.call-start = ((), (), s32[]{:S(2)}) async-start(), calls=%async_computation.14 | async-start | bytes 1310720 | tf_op jit(solution)/shard_map/all_gather | solution.py:181
  107.3 3.4 copy-start.32
  107.3 36.7 %copy-start.11 = (f32[128,1024]{1,0:T(8,128)S(1)}, f32[128,1024]{1,0:T(8,128)}, u32[]{:S(2)}) copy-start(f32[128,1024]{1,0:T(8,128)} %param.26) | copy-start | bytes 1572868
  107.3 42.0 %all-gather.18.cloned.1.call-start = ((), (), s32[]{:S(2)}) async-start(), calls=%async_computation.15 | async-start | bytes 1310720 | tf_op jit(solution)/shard_map/all_gather | solution.py:180
  110.5 34.3 %copy-start.40 = (s32[1,512]{1,0:T(1,128)S(1)}, s32[1,512]{1,0:T(1,128)}, u32[]{:S(2)}) copy-start(s32[1,512]{1,0:T(1,128)} %param.23) | copy-start | bytes 6148
  110.6 56.3 %all-gather.20.cloned.1.call-start = ((), (), s32[]{:S(2)}) async-start(), calls=%async_computation.16 | async-start | bytes 2621440 | tf_op jit(solution)/shard_map/all_gather | solution.py:169
  144.0 74.6 %all-gather.24.cloned.1.call-start = ((), (), s32[]{:S(2)}) async-start(), calls=%async_computation.18 | async-start | bytes 2359296 | tf_op jit(solution)/shard_map/all_gather | solution.py:160
  144.8 91.2 %all-gather.22.cloned.1.call-start = ((), (), s32[]{:S(2)}) async-start(), calls=%async_computation.17 | async-start | bytes 1310720 | tf_op jit(solution)/shard_map/all_gather | solution.py:190
  147.6 3.6 copy-start.22
  149.2 3.2 copy-start.5
  151.2 1.2 copy-start.8
  152.4 2.1 copy-start
  155.7 14.5 %copy-start.26 = (bf16[16,64,128]{2,1,0:T(8,128)(2,1)}, bf16[16,64,128]{2,1,0:T(8,128)(2,1)S(1)}, u32[]{:S(2)}) copy-start(bf16[16,64,128]{2,1,0:T(8,128)(2,1)S(1)} %fusion.32) | copy-start | bytes 786436
  166.9 3.4 copy-start.13
  169.1 2.0 copy-start.41
  170.2 117.6 %all-gather.26.cloned.1.call-start = ((), (), s32[]{:S(2)}) async-start(), calls=%async_computation.19 | async-start | bytes 2359296 | tf_op jit(solution)/shard_map/all_gather | solution.py:161
  171.0 144.1 %reduce-scatter.19.cloned.1.call-start = ((), (), s32[]{:S(2)}) async-start(), calls=%async_computation.20 | async-start | bytes 1310720 | tf_op jit(solution)/shard_map/reduce_scatter | solution.py:193
  240.7 47.1 %copy-start.15 = (bf16[512,1024]{1,0:T(8,128)(2,1)}, bf16[512,1024]{1,0:T(8,128)(2,1)S(1)}, u32[]{:S(2)}) copy-start(bf16[512,1024]{1,0:T(8,128)(2,1)S(1)} %get-tuple-element.74) | copy-start | bytes 3145732
  291.6 25.0 %copy-start.9 = (bf16[1,128,1024]{2,1,0:T(8,128)(2,1)S(1)}, bf16[1,128,1024]{2,1,0:T(8,128)(2,1)}, u32[]{:S(2)}) copy-start(bf16[1,128,1024]{2,1,0:T(8,128)(2,1)} %param.22) | copy-start | bytes 786436
  291.7 43.2 %all-gather.28.cloned.1.call-start = ((), (), s32[]{:S(2)}) async-start(), calls=%async_computation.21 | async-start | bytes 1310720 | tf_op jit(solution)/shard_map/all_gather | solution.py:210
  318.0 49.7 %copy-start.4 = (f32[128,1024]{1,0:T(8,128)}, f32[128,1024]{1,0:T(8,128)S(1)}, u32[]{:S(2)}) copy-start(f32[128,1024]{1,0:T(8,128)S(1)} %get-tuple-element.56) | copy-start | bytes 1572868
  318.0 49.7 %reduce-scatter.21.cloned.1.call-start = ((), (), s32[]{:S(2)}) async-start(), calls=%async_computation.22 | async-start | bytes 1310720 | tf_op jit(solution)/shard_map/reduce_scatter | solution.py:221
  334.9 5.6 copy-start.44
  342.7 27.6 %copy-start.2 = (bf16[1024,1024]{1,0:T(8,128)(2,1)S(1)}, bf16[1024,1024]{1,0:T(8,128)(2,1)}, u32[]{:S(2)}) copy-start(bf16[1024,1024]{1,0:T(8,128)(2,1)} %all-gather.20.cloned.1.call-done) | copy-start | bytes 6291460
  342.7 58.2 %reduce-scatter.39.cloned.1.call-start = ((), (), s32[]{:S(2)}) async-start(), calls=%async_computation.31 | async-start | bytes 1310720
  374.6 1.4 copy-start.6
  376.0 52.3 %reduce-scatter.37.cloned.1.call-start = ((), (), s32[]{:S(2)}) async-start(), calls=%async_computation.30 | async-start | bytes 1310720
  376.0 3.6 copy-start.1
  379.6 1.5 copy-start.23
  382.6 2.4 copy-start.10
  384.9 17.8 %copy-start.27 = (bf16[16,64,128]{2,1,0:T(8,128)(2,1)S(1)}, bf16[16,64,128]{2,1,0:T(8,128)(2,1)}, u32[]{:S(2)}) copy-start(bf16[16,64,128]{2,1,0:T(8,128)(2,1)} %copy-done.26) | copy-start | bytes 786436
  384.9 65.8 %reduce-scatter.35.cloned.1.call-start = ((), (), s32[]{:S(2)}) async-start(), calls=%async_computation.29 | async-start | bytes 20480 | tf_op jit(solution)/shard_map/reduce_scatter | solution.py:277
  402.7 81.6 %reduce-scatter.27.cloned.1.call-start = ((), (), s32[]{:S(2)}) async-start(), calls=%async_computation.25 | async-start | bytes 2621440 | tf_op jit(solution)/shard_map/reduce_scatter | solution.py:274
  404.8 139.9 %reduce-scatter.23.cloned.1.call-start = ((), (), s32[]{:S(2)}) async-start(), calls=%async_computation.23 | async-start | bytes 7864320 | tf_op jit(solution)/shard_map/reduce_scatter | solution.py:271
  428.3 1.8 copy-start.3
  433.4 53.3 %copy-start.18 = (bf16[512,1024]{1,0:T(8,128)(2,1)S(1)}, bf16[512,1024]{1,0:T(8,128)(2,1)}, u32[]{:S(2)}) copy-start(bf16[512,1024]{1,0:T(8,128)(2,1)} %copy-done.17) | copy-start | bytes 3145732
  433.4 53.3 %copy-start.24 = (bf16[512,1024]{1,0:T(8,128)(2,1)S(1)}, bf16[512,1024]{1,0:T(8,128)(2,1)}, u32[]{:S(2)}) copy-start(bf16[512,1024]{1,0:T(8,128)(2,1)} %all-gather.22.cloned.1.call-done) | copy-start | bytes 3145732
  433.4 176.9 %reduce-scatter.41.cloned.1.call-start = ((), (), s32[]{:S(2)}) async-start(), calls=%async_computation.32 | async-start | bytes 147456
  452.2 225.2 %reduce-scatter.29.cloned.1.call-start = ((), (), s32[]{:S(2)}) async-start(), calls=%async_computation.26 | async-start | bytes 1179648 | tf_op jit(solution)/shard_map/reduce_scatter | solution.py:286
  486.4 282.5 %reduce-scatter.31.cloned.1.call-start = ((), (), s32[]{:S(2)}) async-start(), calls=%async_computation.27 | async-start | bytes 4718592 | tf_op jit(solution)/shard_map/reduce_scatter | solution.py:287
  490.0 1.5 copy-start.25
  490.0 371.0 %reduce-scatter.33.cloned.1.call-start = ((), (), s32[]{:S(2)}) async-start(), calls=%async_computation.28 | async-start | bytes 4718592 | tf_op jit(solution)/shard_map/reduce_scatter | solution.py:288
  494.8 444.9 %reduce-scatter.25.cloned.1.call-start = ((), (), s32[]{:S(2)}) async-start(), calls=%async_computation.24 | async-start | bytes 3538944 | tf_op jit(solution)/shard_map/reduce_scatter | solution.py:285
  548.2 1.2 copy-start.45
  548.2 30.9 %copy-start.42 = (f32[128]{0:T(128)S(1)}, f32[128]{0:T(128)}, u32[]{:S(2)}) copy-start(f32[128]{0:T(128)} %param.35) | copy-start | bytes 1540
  548.2 30.9 %copy-start.43 = (f32[128]{0:T(128)S(1)}, f32[128]{0:T(128)}, u32[]{:S(2)}) copy-start(f32[128]{0:T(128)} %param.41) | copy-start | bytes 1540
  581.7 2.1 copy-start.20
  583.8 27.3 %copy-start.38 = (f32[8,32]{1,0:T(8,128)S(1)}, f32[8,32]{1,0:T(8,128)}, u32[]{:S(2)}) copy-start(f32[8,32]{1,0:T(8,128)} %param.34) | copy-start | bytes 3076
  583.8 27.3 %copy-start.39 = (f32[8,32]{1,0:T(8,128)S(1)}, f32[8,32]{1,0:T(8,128)}, u32[]{:S(2)}) copy-start(f32[8,32]{1,0:T(8,128)} %param.40) | copy-start | bytes 3076
  583.8 93.6 %copy-start.33 = (f32[32,1024]{1,0:T(8,128)S(1)}, f32[32,1024]{1,0:T(8,128)}, u32[]{:S(2)}) copy-start(f32[32,1024]{1,0:T(8,128)} %param.25) | copy-start | bytes 393220
  583.9 185.0 %copy-start.12 = (f32[128,1024]{1,0:T(8,128)S(1)}, f32[128,1024]{1,0:T(8,128)}, u32[]{:S(2)}) copy-start(f32[128,1024]{1,0:T(8,128)} %param.26) | copy-start | bytes 1572868
  583.9 185.0 %copy-start.28 = (f32[128,1024]{1,0:T(8,128)S(1)}, f32[128,1024]{1,0:T(8,128)}, u32[]{:S(2)}) copy-start(f32[128,1024]{1,0:T(8,128)} %param.32) | copy-start | bytes 1572868
  583.9 185.0 %copy-start.29 = (f32[128,1024]{1,0:T(8,128)S(1)}, f32[128,1024]{1,0:T(8,128)}, u32[]{:S(2)}) copy-start(f32[128,1024]{1,0:T(8,128)} %param.38) | copy-start | bytes 1572868
  611.1 160.2 %copy-start.36 = (f32[8,32]{1,0:T(8,128)}, f32[8,32]{1,0:T(8,128)S(1)}, u32[]{:S(2)}) copy-start(f32[8,32]{1,0:T(8,128)S(1)} %copy.70) | copy-start | bytes 3076
  611.7 249.2 %copy-start.14 = (f32[128,1024]{1,0:T(8,128)S(1)}, f32[128,1024]{1,0:T(8,128)}, u32[]{:S(2)}) copy-start(f32[128,1024]{1,0:T(8,128)} %param.27) | copy-start | bytes 1572868
  611.7 249.2 %copy-start.30 = (f32[128,1024]{1,0:T(8,128)S(1)}, f32[128,1024]{1,0:T(8,128)}, u32[]{:S(2)}) copy-start(f32[128,1024]{1,0:T(8,128)} %param.33) | copy-start | bytes 1572868
  611.7 249.2 %copy-start.31 = (f32[128,1024]{1,0:T(8,128)S(1)}, f32[128,1024]{1,0:T(8,128)}, u32[]{:S(2)}) copy-start(f32[128,1024]{1,0:T(8,128)} %param.39) | copy-start | bytes 1572868
  771.3 168.3 %copy-start.19 = (f32[3,32,1024]{2,1,0:T(8,128)S(1)}, f32[3,32,1024]{2,1,0:T(8,128)}, u32[]{:S(2)}) copy-start(f32[3,32,1024]{2,1,0:T(8,128)} %param.24) | copy-start | bytes 1179652
  771.3 168.3 %copy-start.34 = (f32[3,32,1024]{2,1,0:T(8,128)S(1)}, f32[3,32,1024]{2,1,0:T(8,128)}, u32[]{:S(2)}) copy-start(f32[3,32,1024]{2,1,0:T(8,128)} %param.30) | copy-start | bytes 1179652
  771.3 168.3 %copy-start.35 = (f32[3,32,1024]{2,1,0:T(8,128)S(1)}, f32[3,32,1024]{2,1,0:T(8,128)}, u32[]{:S(2)}) copy-start(f32[3,32,1024]{2,1,0:T(8,128)} %param.36) | copy-start | bytes 1179652
  (4 other events, 3.8 us)
Sparse Core Ops, SparseCore 0:
  10.8 46.9 all-gather.11
  59.3 44.7 all-gather.13
  107.4 16.6 all-gather.15
  126.1 16.6 all-gather.17
  144.3 22.5 all-gather.19
  169.4 49.1 all-gather.23
  220.7 15.2 all-gather.21
  238.7 49.0 all-gather.25
  291.8 23.2 reduce-scatter.18
  318.1 16.7 all-gather.27
  342.9 24.7 reduce-scatter.20
  376.1 24.8 reduce-scatter.38
  403.5 24.7 reduce-scatter.36
  431.1 19.5 reduce-scatter.34
  453.1 31.1 reduce-scatter.26
  486.7 57.9 reduce-scatter.22
  548.4 61.8 reduce-scatter.40
  614.2 63.2 reduce-scatter.28
  681.6 87.2 reduce-scatter.30
  772.9 87.9 reduce-scatter.32
  865.2 74.4 reduce-scatter.24
where the time goes:
time: 950 us; the launch traced here: 949 us
  waiting for transfers between devices  709 us (75%)
  blocking collectives  113 us (12%)
  matrix products  60.1 us (6%)
  other arithmetic  31.5 us (3%)
  local copies, waits for them, and re-layouts  17.5 us (2%)
  between operations  16.4 us (2%)
    reduce_scatter x1, waiting for transfers between devices, body(): lax.psum_scatter(expand_part, 'rep', scatter_dimension=0, tiled=True)  89.6 us
    reduce_scatter x1, waiting for transfers between devices, body(): lax.psum_scatter(shrink_part, 'rep', scatter_dimension=0, tiled=True)  89.6 us
    reduce_scatter x1, waiting for transfers between devices, body(): lax.psum_scatter(intake_part, 'rep', scatter_dimension=1, tiled=True)  76.2 us
    reduce_scatter x1, waiting for transfers between devices, body(): lax.psum_scatter(outlet_part, 'rep', scatter_dimension=0, tiled=True)  65.7 us
    unnamed x24, waiting for transfers between devices  58 us
    reduce_scatter x1, waiting for transfers between devices, body(): lax.psum_scatter(intake_full.astype(jnp.bfloat16), 'shard', scatter_dimen...  49.8 us
    all_gather x1, waiting for transfers between devices, body(): lax.all_gather(intake.astype(jnp.bfloat16), 'rep', axis=1, tiled=True)  48.7 us
    all_gather x1, waiting for transfers between devices, body(): lax.all_gather(shrink.astype(jnp.bfloat16), 'rep', axis=0, tiled=True)  47.1 us
  transfers between devices with their start and end apart: 21, of which 19 were waited for; matrix products, arithmetic and copies ran while one was open for 8% of the time, Pallas kernels for 0%

commit v1 on v0

--- a/solution.py
+++ b/solution.py
@@ -12,6 +12,27 @@
 weight_decay = 0.1
 step_count = 3
 norm_eps = 1e-05
+
+
+def in_order(pieces, dim):
+    dims = list(pieces.shape[1:])
+    dims[dim] *= pieces.shape[0]
+    return jnp.moveaxis(pieces, 0, dim).reshape(dims)
+
+
+def grow_blocks(x, axis):
+    peers, position = (lax.axis_size(axis), lax.axis_index(axis))
+    blocks, distance = (x[None], 1)
+    while distance < peers:
+        other = lax.ppermute(blocks, axis, [(i, i ^ distance) for i in range(peers)])
+        low = position & distance == 0
+        blocks = jnp.concatenate([jnp.where(low, blocks, other), jnp.where(low, other, blocks)])
+        distance *= 2
+    return blocks
+
+
+def gather_by_bits(x, axis, dim):
+    return in_order(grow_blocks(x, axis), dim)
 
 
 def layer_norm(values_in):
@@ -155,7 +176,7 @@
     every_seg = segment_ids.reshape(seq_len)
     own_seg = lax.dynamic_slice_in_dim(every_seg, position * own_rows, own_rows)
     part_intake, part_outlet, part_expand, part_shrink, part_affine, part_offset = (
-        lax.all_gather(intake.astype(jnp.bfloat16), "rep", axis=1, tiled=True),
+        gather_by_bits(intake.astype(jnp.bfloat16), "rep", 1),
         lax.all_gather(outlet.astype(jnp.bfloat16), "rep", axis=0, tiled=True),
         lax.all_gather(expand.astype(jnp.bfloat16), "rep", axis=0, tiled=True),
         lax.all_gather(shrink.astype(jnp.bfloat16), "rep", axis=0, tiled=True),

time: 950 us -> 987 us (1.039)
  waiting for transfers between devices: 709 us -> 738 us
    all_gather x1 -> x0, waiting for transfers between devices: 48.7 us -> none  [body(): lax.all_gather(intake.astype(jnp.bfloat16), 'rep', axis=1, tiled=True)]
    ppermute x0 -> x3, waiting for transfers between devices: none -> 46.5 us  [grow_blocks(): lax.ppermute(blocks, axis, [(i, i ^ distance) for i in range(peers)])]
    all_gather x1, waiting for transfers between devices: 14.7 us -> 47.2 us  [layer_params(): lax.all_gather(part_intake, 'shard', axis=1, tiled=True)]
    unnamed x24 -> x23, waiting for transfers between devices: 58 us -> 57.7 us
  transfers between devices with their start and end apart: 21 -> 23, of which waited for: 19 -> 21; matrix products, arithmetic and copies ran while one was open for 8% -> 8% of each run, Pallas kernels for 0% -> 0%
where the time goes in v1:
time: 987 us; the launch traced here: 986 us
  waiting for transfers between devices  738 us (75%)
  blocking collectives  113 us (11%)
  matrix products  65.4 us (7%)
  other arithmetic  33.3 us (3%)
  between operations  16.3 us (2%)
  local copies, waits for them, and re-layouts  11.8 us (1%)
    reduce_scatter x1, waiting for transfers between devices, body(): lax.psum_scatter(shrink_part, 'rep', scatter_dimension=0, tiled=True)  89.7 us
    reduce_scatter x1, waiting for transfers between devices, body(): lax.psum_scatter(expand_part, 'rep', scatter_dimension=0, tiled=True)  89.5 us
    reduce_scatter x1, waiting for transfers between devices, body(): lax.psum_scatter(intake_part, 'rep', scatter_dimension=1, tiled=True)  76.1 us
    reduce_scatter x1, waiting for transfers between devices, body(): lax.psum_scatter(outlet_part, 'rep', scatter_dimension=0, tiled=True)  65.6 us
    unnamed x23, waiting for transfers between devices  57.7 us
    reduce_scatter x1, waiting for transfers between devices, body(): lax.psum_scatter(intake_full.astype(jnp.bfloat16), 'shard', scatter_dimen...  49.8 us
    all_gather x1, waiting for transfers between devices, layer_params(): lax.all_gather(part_intake, 'shard', axis=1, tiled=True)  47.2 us
    all_gather x1, waiting for transfers between devices, body(): lax.all_gather(shrink.astype(jnp.bfloat16), 'rep', axis=0, tiled=True)  47.1 us
  transfers between devices with their start and end apart: 23, of which 21 were waited for; matrix products, arithmetic and copies ran while one was open for 8% of the time, Pallas kernels for 0%

profile of v1, /device:TPU:0, one launch (start us, length us, event | category | flops | bytes accessed | tf_op | source)
XLA Modules:
  0.0 986.0 jit_solution(13118711143362918365)
XLA Ops:
  8.3 3.1 collective-permute-start
  11.3 4.9 collective-permute-done
  17.3 1.9 collective-permute-start.1
  19.2 8.5 collective-permute-done.1
  27.8 2.6 collective-permute-start.2
  30.4 33.1 %collective-permute-done.2 = bf16[4,3,32,1024]{3,2,0,1:T(8,128)(2,1)S(1)} collective-permute-done((bf16[4,3,32,1024]{3,2,0,1:T(8,128)(2,1)S(1)}, bf16[4,3,32,1024]{3,2,0,1:T(8,128)(2,1)S(1)}, u32[]{:S(2)}, u32[]{:S(2)}) %collective-permute-start.2) | collective-permute-done | bytes 786464 | tf_op jit(solution)/shard_map/ppermute | solution.py:27
  65.0 47.2 %all-gather.11.cloned.1.call-done = bf16[3,1024,1024]{2,1,0:T(8,128)(2,1)} async-done(((bf16[3,256,1024]{2,1,0:T(8,128)(2,1)}), bf16[3,1024,1024]{2,1,0:T(8,128)(2,1)}) %all-gather.11.cloned.1.call-update) | async-done | bytes 6291472 | tf_op jit(solution)/shard_map/all_gather | solution.py:189
  112.2 3.0 fusion.36
  115.3 26.2 %all-gather = bf16[8,32,8]{1,2,0:T(8,128)(2,1)S(1)} all-gather(bf16[1,32,8]{1,2,0:T(8,128)(2,1)S(1)} %convert_bitcast_fusion.4), channel_id=1, replica_groups=mesh['shard'=4,'rep'=8] {'rep'}, dimensions={0}, use_global_device_ids=true | all-gather | bytes 4608 | tf_op jit(solution)/shard_map/all_gather | solution.py:183
  141.6 5.2 all_gather.41
  146.8 3.1 fusion.35
  150.0 33.4 %all_gather.44 = bf16[256,1024]{1,0:T(8,128)(2,1)} all-gather(bf16[32,1024]{1,0:T(8,128)(2,1)S(1)} %convert_element_type.171), channel_id=1, replica_groups=mesh['shard'=4,'rep'=8] {'rep'}, dimensions={0}, use_global_device_ids=true | all-gather | bytes 589824 | tf_op jit(solution)/shard_map/all_gather | solution.py:180
  184.4 2.3 fusion.34
  186.8 4.4 fusion
  191.2 3.7 fusion.32
  194.9 9.7 all-gather.17.cloned.1.call-done
  204.6 2.2 fusion.81
  208.9 20.5 %all-gather.1 = bf16[8,1,128]{2,1,0:T(2,128)(2,1)S(1)} all-gather(bf16[1,1,128]{2,1,0:T(2,128)(2,1)S(1)} %convert_bitcast_fusion.5), channel_id=1, replica_groups=mesh['shard'=4,'rep'=8] {'rep'}, dimensions={0}, use_global_device_ids=true | all-gather | bytes 2304 | tf_op jit(solution)/shard_map/all_gather | solution.py:184
  229.4 27.0 %all-gather.21.cloned.1.call-done = bf16[1024,1024]{1,0:T(8,128)(2,1)} async-done(((bf16[128,1024]{1,0:T(8,128)(2,1)}), bf16[1024,1024]{1,0:T(8,128)(2,1)}) %all-gather.21.cloned.1.call-update) | async-done | bytes 2097168 | tf_op jit(solution)/shard_map/all_gather | solution.py:181
  256.3 17.2 %all-gather.19.cloned.1.call-done = bf16[512,1024]{1,0:T(8,128)(2,1)} async-done(((bf16[128,1024]{1,0:T(8,128)(2,1)}), bf16[512,1024]{1,0:T(8,128)(2,1)}) %all-gather.19.cloned.1.call-update) | async-done | bytes 1048592 | tf_op jit(solution)/shard_map/all_gather | solution.py:211
  273.6 4.7 multiply_convert_fusion.2
  278.3 47.1 %all-gather.23.cloned.1.call-done = bf16[1024,1024]{1,0:T(8,128)(2,1)} async-done(((bf16[128,1024]{1,0:T(8,128)(2,1)}), bf16[1024,1024]{1,0:T(8,128)(2,1)}) %all-gather.23.cloned.1.call-update) | async-done | bytes 2097168 | tf_op jit(solution)/shard_map/all_gather | solution.py:182
  325.4 3.8 convolution_convert_fusion.2
  329.3 23.4 %reduce-scatter.19.cloned.1.call-done = bf16[128,1024]{1,0:T(8,128)(2,1)} async-done(((bf16[512,1024]{1,0:T(8,128)(2,1)}), bf16[128,1024]{1,0:T(8,128)(2,1)}) %reduce-scatter.19.cloned.1.call-update) | async-done | bytes 262160 | tf_op jit(solution)/shard_map/reduce_scatter | solution.py:214
  355.8 16.6 %all-gather.25.cloned.1.call-done = bf16[512,1024]{1,0:T(8,128)(2,1)} async-done(((bf16[128,1024]{1,0:T(8,128)(2,1)}), bf16[512,1024]{1,0:T(8,128)(2,1)}) %all-gather.25.cloned.1.call-update) | async-done | bytes 1048592 | tf_op jit(solution)/shard_map/all_gather | solution.py:231
  372.5 4.6 fusion.82
  378.1 2.3 convolution_convert_fusion.1
  380.4 24.9 %reduce-scatter.21.cloned.1.call-done = bf16[128,1024]{1,0:T(8,128)(2,1)} async-done(((bf16[512,1024]{1,0:T(8,128)(2,1)}), bf16[128,1024]{1,0:T(8,128)(2,1)}) %reduce-scatter.21.cloned.1.call-update) | async-done | bytes 262160 | tf_op jit(solution)/shard_map/reduce_scatter | solution.py:242
  406.6 1.3 fusion.75
  409.0 3.3 fusion.20
  412.2 1.3 copy.55
  413.7 3.5 multiply_reduce_fusion
  417.3 1.5 multiply_convert_fusion
  418.8 1.4 multiply_convert_fusion.1
  420.2 2.3 copy.53
  422.7 2.1 fusion.79
  425.0 13.6 %reduce-scatter.39.cloned.1.call-done = bf16[128,1024]{1,0:T(8,128)(2,1)} async-done(((bf16[512,1024]{1,0:T(8,128)(2,1)}), bf16[128,1024]{1,0:T(8,128)(2,1)}) %reduce-scatter.39.cloned.1.call-update) | async-done | bytes 262160
  440.3 2.0 convolution_convert_fusion
  443.2 2.1 convert_bitcast_fusion
  445.4 20.3 %reduce-scatter.37.cloned.1.call-done = bf16[128,1024]{1,0:T(8,128)(2,1)} async-done(((bf16[512,1024]{1,0:T(8,128)(2,1)}), bf16[128,1024]{1,0:T(8,128)(2,1)}) %reduce-scatter.37.cloned.1.call-update) | async-done | bytes 262160
  465.7 1.8 convert_bitcast_fusion.1
  467.5 3.3 pad_maximum_fusion
  470.9 17.4 %reduce-scatter.35.cloned.1.call-done = bf16[8,256]{1,0:T(8,128)(2,1)} async-done(((bf16[8,1024]{1,0:T(8,128)(2,1)}), bf16[8,256]{1,0:T(8,128)(2,1)}) %reduce-scatter.35.cloned.1.call-update) | async-done | bytes 4112 | tf_op jit(solution)/shard_map/reduce_scatter | solution.py:298
  488.3 1.4 copy.57
  489.8 32.1 %reduce-scatter.27.cloned.1.call-done = bf16[256,1024]{1,0:T(8,128)(2,1)} async-done(((bf16[1024,1024]{1,0:T(8,128)(2,1)}), bf16[256,1024]{1,0:T(8,128)(2,1)}) %reduce-scatter.27.cloned.1.call-update) | async-done | bytes 524304 | tf_op jit(solution)/shard_map/reduce_scatter | solution.py:295
  521.8 2.1 convert_element_type.202
  524.3 3.2 fusion.47
  529.0 3.3 fusion.83
  532.4 49.8 %reduce-scatter.23.cloned.1.call-done = bf16[3,256,1024]{2,1,0:T(8,128)(2,1)} async-done(((bf16[3,1024,1024]{2,1,0:T(8,128)(2,1)}), bf16[3,256,1024]{2,1,0:T(8,128)(2,1)}) %reduce-scatter.23.cloned.1.call-update) | async-done | bytes 1572880 | tf_op jit(solution)/shard_map/reduce_scatter | solution.py:292
  582.2 3.5 convert_element_type.200
  589.1 5.8 all-reduce
  594.9 21.6 %all-reduce.1 = f32[1024]{0:T(1024)S(1)} all-reduce(f32[1024]{0:T(1024)S(1)} %dynamic-slice_convert_fusion), channel_id=15, replica_groups=mesh['shard'=4,'rep'=8] {'rep'}, use_global_device_ids=true, to_apply=%region_32.33.clone | all-reduce | flops 1024 | bytes 8192
  617.2 2.1 fusion.27
  619.3 2.1 fusion.14
  621.4 2.9 fusion.37
  624.3 23.5 %reduce-scatter.41.cloned.1.call-done = f32[32,8]{1,0:T(8,128)} async-done(((f32[256,8]{1,0:T(8,128)}), f32[32,8]{1,0:T(8,128)}) %reduce-scatter.41.cloned.1.call-update) | async-done | bytes 1040
  649.3 65.6 %reduce-scatter.29.cloned.1.call-done = f32[32,1024]{1,0:T(8,128)} async-done(((f32[256,1024]{1,0:T(8,128)}), f32[32,1024]{1,0:T(8,128)}) %reduce-scatter.29.cloned.1.call-update) | async-done | bytes 131088 | tf_op jit(solution)/shard_map/reduce_scatter | solution.py:307
  714.9 1.8 multiply_subtract_fusion.3
  716.7 89.5 %reduce-scatter.31.cloned.1.call-done = f32[128,1024]{1,0:T(8,128)} async-done(((f32[1024,1024]{1,0:T(8,128)}), f32[128,1024]{1,0:T(8,128)}) %reduce-scatter.31.cloned.1.call-update) | async-done | bytes 524304 | tf_op jit(solution)/shard_map/reduce_scatter | solution.py:308
  806.2 2.4 multiply_subtract_fusion.1
  808.7 89.7 %reduce-scatter.33.cloned.1.call-done = f32[128,1024]{1,0:T(8,128)} async-done(((f32[1024,1024]{1,0:T(8,128)}), f32[128,1024]{1,0:T(8,128)}) %reduce-scatter.33.cloned.1.call-update) | async-done | bytes 524304 | tf_op jit(solution)/shard_map/reduce_scatter | solution.py:309
  898.4 2.4 multiply_subtract_fusion
  900.8 76.1 %reduce-scatter.25.cloned.1.call-done = f32[3,32,1024]{2,1,0:T(8,128)} async-done(((f32[3,256,1024]{2,1,0:T(8,128)}), f32[3,32,1024]{2,1,0:T(8,128)}) %reduce-scatter.25.cloned.1.call-update) | async-done | bytes 393232 | tf_op jit(solution)/shard_map/reduce_scatter | solution.py:306
  977.0 2.2 multiply_subtract_fusion.2
  (187 shorter events, 22.5 us)
Async XLA Ops:
  7.2 105.0 %all-gather.11.cloned.1.call-start = ((), (), s32[]{:S(2)}) async-start(), calls=%async_computation.12 | async-start | bytes 7864320 | tf_op jit(solution)/shard_map/all_gather | solution.py:189
  8.3 8.0 collective-permute-start
  17.3 10.3 %collective-permute-start.1 = (bf16[2,3,32,1024]{3,2,0,1:T(8,128)(2,1)S(1)}, bf16[2,3,32,1024]{3,2,0,1:T(8,128)(2,1)S(1)}, u32[]{:S(2)}, u32[]{:S(2)}) collective-permute-start(bf16[2,3,32,1024]{3,2,0,1:T(8,128)(2,1)S(1)} %pad_maximum_fusion.3), channel_id=1, source_target_pairs={{0,2},{1,3},{2,0},{3,1},{4,6},{5,7},{6,4},{7,5},{8,10},{9,11},{10,... | collective-permute-start | bytes 1179656 | tf_op jit(solution)/shard_map/ppermute | solution.py:27
  27.8 35.7 %collective-permute-start.2 = (bf16[4,3,32,1024]{3,2,0,1:T(8,128)(2,1)S(1)}, bf16[4,3,32,1024]{3,2,0,1:T(8,128)(2,1)S(1)}, u32[]{:S(2)}, u32[]{:S(2)}) collective-permute-start(bf16[4,3,32,1024]{3,2,0,1:T(8,128)(2,1)S(1)} %pad_maximum_fusion.2), channel_id=1, source_target_pairs={{0,4},{1,5},{2,6},{3,7},{4,0},{5,1},{6,2},{7,3},{8,12},{9,13},{10,... | collective-permute-start | bytes 2359304 | tf_op jit(solution)/shard_map/ppermute | solution.py:27
  63.6 48.6 %copy-start.4 = (bf16[1,128,1024]{2,1,0:T(8,128)(2,1)S(1)}, bf16[1,128,1024]{2,1,0:T(8,128)(2,1)}, u32[]{:S(2)}) copy-start(bf16[1,128,1024]{2,1,0:T(8,128)(2,1)} %param.21) | copy-start | bytes 786436
  64.9 50.4 %copy-start.34 = (f32[8,32]{1,0:T(8,128)S(1)}, f32[8,32]{1,0:T(8,128)}, u32[]{:S(2)}) copy-start(f32[8,32]{1,0:T(8,128)} %param.28) | copy-start | bytes 3076
  64.9 121.9 %all-gather.15.cloned.1.call-start = ((), (), s32[]{:S(2)}) async-start(), calls=%async_computation.14 | async-start | bytes 1310720 | tf_op jit(solution)/shard_map/all_gather | solution.py:201
  115.2 34.7 %copy-start.27 = (f32[32,1024]{1,0:T(8,128)S(1)}, f32[32,1024]{1,0:T(8,128)}, u32[]{:S(2)}) copy-start(f32[32,1024]{1,0:T(8,128)} %param.25) | copy-start | bytes 393220
  115.2 76.0 %all-gather.13.cloned.1.call-start = ((), (), s32[]{:S(2)}) async-start(), calls=%async_computation.13 | async-start | bytes 1310720 | tf_op jit(solution)/shard_map/all_gather | solution.py:202
  146.8 36.6 %copy-start.8 = (f32[128,1024]{1,0:T(8,128)S(1)}, f32[128,1024]{1,0:T(8,128)}, u32[]{:S(2)}) copy-start(f32[128,1024]{1,0:T(8,128)} %param.26) | copy-start | bytes 1572868
  149.9 34.4 %copy-start.37 = (s32[1,512]{1,0:T(1,128)S(1)}, s32[1,512]{1,0:T(1,128)}, u32[]{:S(2)}) copy-start(s32[1,512]{1,0:T(1,128)} %param.23) | copy-start | bytes 6148
  149.9 54.7 %all-gather.17.cloned.1.call-start = ((), (), s32[]{:S(2)}) async-start(), calls=%async_computation.15 | async-start | bytes 2621440 | tf_op jit(solution)/shard_map/all_gather | solution.py:190
  183.4 73.0 %all-gather.21.cloned.1.call-start = ((), (), s32[]{:S(2)}) async-start(), calls=%async_computation.17 | async-start | bytes 2359296 | tf_op jit(solution)/shard_map/all_gather | solution.py:181
  184.2 89.4 %all-gather.19.cloned.1.call-start = ((), (), s32[]{:S(2)}) async-start(), calls=%async_computation.16 | async-start | bytes 1310720 | tf_op jit(solution)/shard_map/all_gather | solution.py:211
  186.7 4.5 copy-start.31
  194.9 13.0 %copy-start.21 = (bf16[16,64,128]{2,1,0:T(8,128)(2,1)}, bf16[16,64,128]{2,1,0:T(8,128)(2,1)S(1)}, u32[]{:S(2)}) copy-start(bf16[16,64,128]{2,1,0:T(8,128)(2,1)S(1)} %fusion.32) | copy-start | bytes 786436
  204.6 3.4 copy-start.10
  206.8 2.0 copy-start.38
  208.0 117.4 %all-gather.23.cloned.1.call-start = ((), (), s32[]{:S(2)}) async-start(), calls=%async_computation.18 | async-start | bytes 2359296 | tf_op jit(solution)/shard_map/all_gather | solution.py:182
  208.8 143.9 %reduce-scatter.19.cloned.1.call-start = ((), (), s32[]{:S(2)}) async-start(), calls=%async_computation.19 | async-start | bytes 1310720 | tf_op jit(solution)/shard_map/reduce_scatter | solution.py:214
  278.3 47.1 %copy-start.12 = (bf16[512,1024]{1,0:T(8,128)(2,1)}, bf16[512,1024]{1,0:T(8,128)(2,1)S(1)}, u32[]{:S(2)}) copy-start(bf16[512,1024]{1,0:T(8,128)(2,1)S(1)} %get-tuple-element.80) | copy-start | bytes 3145732
  329.2 25.0 %copy-start.6 = (bf16[1,128,1024]{2,1,0:T(8,128)(2,1)S(1)}, bf16[1,128,1024]{2,1,0:T(8,128)(2,1)}, u32[]{:S(2)}) copy-start(bf16[1,128,1024]{2,1,0:T(8,128)(2,1)} %param.22) | copy-start | bytes 786436
  329.3 43.2 %all-gather.25.cloned.1.call-start = ((), (), s32[]{:S(2)}) async-start(), calls=%async_computation.20 | async-start | bytes 1310720 | tf_op jit(solution)/shard_map/all_gather | solution.py:231
  355.6 49.8 %copy-start.3 = (f32[128,1024]{1,0:T(8,128)}, f32[128,1024]{1,0:T(8,128)S(1)}, u32[]{:S(2)}) copy-start(f32[128,1024]{1,0:T(8,128)S(1)} %get-tuple-element.56) | copy-start | bytes 1572868
  355.6 49.7 %reduce-scatter.21.cloned.1.call-start = ((), (), s32[]{:S(2)}) async-start(), calls=%async_computation.21 | async-start | bytes 1310720 | tf_op jit(solution)/shard_map/reduce_scatter | solution.py:242
  372.5 5.6 copy-start.41
  380.3 27.6 %copy-start.1 = (bf16[1024,1024]{1,0:T(8,128)(2,1)S(1)}, bf16[1024,1024]{1,0:T(8,128)(2,1)}, u32[]{:S(2)}) copy-start(bf16[1024,1024]{1,0:T(8,128)(2,1)} %all-gather.17.cloned.1.call-done) | copy-start | bytes 6291460
  380.3 58.2 %reduce-scatter.39.cloned.1.call-start = ((), (), s32[]{:S(2)}) async-start(), calls=%async_computation.30 | async-start | bytes 1310720
  412.2 1.4 copy-start.17
  413.6 52.1 %reduce-scatter.37.cloned.1.call-start = ((), (), s32[]{:S(2)}) async-start(), calls=%async_computation.29 | async-start | bytes 1310720
  413.7 3.6 copy-start
  417.2 1.5 copy-start.32
  420.2 2.4 copy-start.7
  422.5 17.8 %copy-start.22 = (bf16[16,64,128]{2,1,0:T(8,128)(2,1)S(1)}, bf16[16,64,128]{2,1,0:T(8,128)(2,1)}, u32[]{:S(2)}) copy-start(bf16[16,64,128]{2,1,0:T(8,128)(2,1)} %copy-done.21) | copy-start | bytes 786436
  422.5 65.7 %reduce-scatter.35.cloned.1.call-start = ((), (), s32[]{:S(2)}) async-start(), calls=%async_computation.28 | async-start | bytes 20480 | tf_op jit(solution)/shard_map/reduce_scatter | solution.py:298
  440.2 81.6 %reduce-scatter.27.cloned.1.call-start = ((), (), s32[]{:S(2)}) async-start(), calls=%async_computation.24 | async-start | bytes 2621440 | tf_op jit(solution)/shard_map/reduce_scatter | solution.py:295
  442.3 139.9 %reduce-scatter.23.cloned.1.call-start = ((), (), s32[]{:S(2)}) async-start(), calls=%async_computation.22 | async-start | bytes 7864320 | tf_op jit(solution)/shard_map/reduce_scatter | solution.py:292
  465.7 1.8 copy-start.2
  470.8 53.4 %copy-start.15 = (bf16[512,1024]{1,0:T(8,128)(2,1)S(1)}, bf16[512,1024]{1,0:T(8,128)(2,1)}, u32[]{:S(2)}) copy-start(bf16[512,1024]{1,0:T(8,128)(2,1)} %copy-done.14) | copy-start | bytes 3145732
  470.8 53.4 %copy-start.19 = (bf16[512,1024]{1,0:T(8,128)(2,1)S(1)}, bf16[512,1024]{1,0:T(8,128)(2,1)}, u32[]{:S(2)}) copy-start(bf16[512,1024]{1,0:T(8,128)(2,1)} %all-gather.19.cloned.1.call-done) | copy-start | bytes 3145732
  470.8 177.0 %reduce-scatter.41.cloned.1.call-start = ((), (), s32[]{:S(2)}) async-start(), calls=%async_computation.31 | async-start | bytes 147456
  489.7 225.2 %reduce-scatter.29.cloned.1.call-start = ((), (), s32[]{:S(2)}) async-start(), calls=%async_computation.25 | async-start | bytes 1179648 | tf_op jit(solution)/shard_map/reduce_scatter | solution.py:307
  524.0 282.2 %reduce-scatter.31.cloned.1.call-start = ((), (), s32[]{:S(2)}) async-start(), calls=%async_computation.26 | async-start | bytes 4718592 | tf_op jit(solution)/shard_map/reduce_scatter | solution.py:308
  527.5 1.2 copy-start.13
  527.5 1.5 copy-start.20
  527.5 370.9 %reduce-scatter.33.cloned.1.call-start = ((), (), s32[]{:S(2)}) async-start(), calls=%async_computation.27 | async-start | bytes 4718592 | tf_op jit(solution)/shard_map/reduce_scatter | solution.py:309
  532.3 444.7 %reduce-scatter.25.cloned.1.call-start = ((), (), s32[]{:S(2)}) async-start(), calls=%async_computation.23 | async-start | bytes 3538944 | tf_op jit(solution)/shard_map/reduce_scatter | solution.py:306
  585.7 1.2 copy-start.42
  585.7 30.9 %copy-start.39 = (f32[128]{0:T(128)S(1)}, f32[128]{0:T(128)}, u32[]{:S(2)}) copy-start(f32[128]{0:T(128)} %param.35) | copy-start | bytes 1540
  585.7 30.9 %copy-start.40 = (f32[128]{0:T(128)S(1)}, f32[128]{0:T(128)}, u32[]{:S(2)}) copy-start(f32[128]{0:T(128)} %param.41) | copy-start | bytes 1540
  619.3 2.1 copy-start.16
  621.4 27.3 %copy-start.35 = (f32[8,32]{1,0:T(8,128)S(1)}, f32[8,32]{1,0:T(8,128)}, u32[]{:S(2)}) copy-start(f32[8,32]{1,0:T(8,128)} %param.34) | copy-start | bytes 3076
  621.4 27.2 %copy-start.36 = (f32[8,32]{1,0:T(8,128)S(1)}, f32[8,32]{1,0:T(8,128)}, u32[]{:S(2)}) copy-start(f32[8,32]{1,0:T(8,128)} %param.40) | copy-start | bytes 3076
  621.4 93.5 %copy-start.28 = (f32[32,1024]{1,0:T(8,128)S(1)}, f32[32,1024]{1,0:T(8,128)}, u32[]{:S(2)}) copy-start(f32[32,1024]{1,0:T(8,128)} %param.25) | copy-start | bytes 393220
  621.4 184.8 %copy-start.9 = (f32[128,1024]{1,0:T(8,128)S(1)}, f32[128,1024]{1,0:T(8,128)}, u32[]{:S(2)}) copy-start(f32[128,1024]{1,0:T(8,128)} %param.26) | copy-start | bytes 1572868
  621.4 184.8 %copy-start.23 = (f32[128,1024]{1,0:T(8,128)S(1)}, f32[128,1024]{1,0:T(8,128)}, u32[]{:S(2)}) copy-start(f32[128,1024]{1,0:T(8,128)} %param.32) | copy-start | bytes 1572868
  621.4 184.8 %copy-start.24 = (f32[128,1024]{1,0:T(8,128)S(1)}, f32[128,1024]{1,0:T(8,128)}, u32[]{:S(2)}) copy-start(f32[128,1024]{1,0:T(8,128)} %param.38) | copy-start | bytes 1572868
  648.6 160.1 %copy-start.33 = (f32[8,32]{1,0:T(8,128)}, f32[8,32]{1,0:T(8,128)S(1)}, u32[]{:S(2)}) copy-start(f32[8,32]{1,0:T(8,128)S(1)} %copy.58) | copy-start | bytes 3076
  649.2 249.1 %copy-start.11 = (f32[128,1024]{1,0:T(8,128)S(1)}, f32[128,1024]{1,0:T(8,128)}, u32[]{:S(2)}) copy-start(f32[128,1024]{1,0:T(8,128)} %param.27) | copy-start | bytes 1572868
  649.3 249.1 %copy-start.25 = (f32[128,1024]{1,0:T(8,128)S(1)}, f32[128,1024]{1,0:T(8,128)}, u32[]{:S(2)}) copy-start(f32[128,1024]{1,0:T(8,128)} %param.33) | copy-start | bytes 1572868
  649.3 249.1 %copy-start.26 = (f32[128,1024]{1,0:T(8,128)S(1)}, f32[128,1024]{1,0:T(8,128)}, u32[]{:S(2)}) copy-start(f32[128,1024]{1,0:T(8,128)} %param.39) | copy-start | bytes 1572868
  808.7 168.3 %copy-start.5 = (f32[3,32,1024]{2,1,0:T(8,128)S(1)}, f32[3,32,1024]{2,1,0:T(8,128)}, u32[]{:S(2)}) copy-start(f32[3,32,1024]{2,1,0:T(8,128)} %param.24) | copy-start | bytes 1179652
  808.7 168.3 %copy-start.29 = (f32[3,32,1024]{2,1,0:T(8,128)S(1)}, f32[3,32,1024]{2,1,0:T(8,128)}, u32[]{:S(2)}) copy-start(f32[3,32,1024]{2,1,0:T(8,128)} %param.30) | copy-start | bytes 1179652
  808.7 168.3 %copy-start.30 = (f32[3,32,1024]{2,1,0:T(8,128)S(1)}, f32[3,32,1024]{2,1,0:T(8,128)}, u32[]{:S(2)}) copy-start(f32[3,32,1024]{2,1,0:T(8,128)} %param.36) | copy-start | bytes 1179652
  (3 other events, 2.6 us)
Sparse Core Ops, SparseCore 0:
  65.0 47.1 all-gather.10
  115.4 16.8 all-gather.14
  150.0 15.2 all-gather.12
  183.5 21.0 all-gather.16
  207.2 49.1 all-gather.20
  258.3 15.2 all-gather.18
  276.3 49.0 all-gather.22
  329.4 23.2 reduce-scatter.18
  355.7 16.7 all-gather.24
  380.5 24.8 reduce-scatter.20
  413.7 24.7 reduce-scatter.38
  440.9 24.7 reduce-scatter.36
  468.7 19.5 reduce-scatter.34
  490.6 31.1 reduce-scatter.26
  524.2 57.9 reduce-scatter.22
  585.9 61.8 reduce-scatter.40
  651.7 63.1 reduce-scatter.28
  719.0 87.2 reduce-scatter.30
  810.4 87.9 reduce-scatter.32
  902.4 74.5 reduce-scatter.24
